TPU v7x, 128 devices: a whole 4x4x4 slice. The times are simulated.
128 devices in a mesh: expert: 64 (over y, x, z), zero: 2 (over core).
Axes of the slice: x: 4, y: 4, z: 4, core: 2. Of those that a mesh axis runs over, the one named last changes fastest.
Arguments:
- tokens: bfloat16 [8192, 7168], P(('expert', 'zero')), may hold values from -6 to 6
- expert_ids: int32 [8192, 8], P(('expert', 'zero')), may hold values from 0 to 63, all different within a row; in each aligned block of 64 rows (0 to 63, 64 to 127, ...) at most 10 rows name the same one
- gate_logits: float32 [8192, 8], P(('expert', 'zero')), may hold values from -6 to 6
- w_gate: bfloat16 [64, 7168, 1024], P('expert', 'zero'), may hold values from -0.0625 to 0.0625
- w_up: bfloat16 [64, 7168, 1024], P('expert', 'zero'), may hold values from -0.0625 to 0.0625
- w_down: bfloat16 [64, 1024, 7168], P('expert', None, 'zero'), may hold values from -0.1875 to 0.1875
Outputs:
- moe_out: bfloat16 [8192, 7168], P(('expert', 'zero'))
Inputs may be any that keep to these rules, and one draw needn't show every extreme that they name: `expert_ids`: in each aligned block of 64 tokens (the tokens of one device) no expert is named by more than 10 tokens, and in some block one expert is named by exactly 10. Each token names 8 different experts, and every expert is named somewhere.
All inputs are finite; a program needn't handle non-finite values.
Results may differ from a plain program's by a relative error of at most 0.0059.
Values may be sent and summed in bfloat16 or wider, within the bound.
No kernel may reach another device: no remote copies, remote signals or barrier semaphores. Data moves between devices by JAX's collectives and lax.ppermute only.
A program may use at most 256 MiB of HBM per device.

v0:
```python
import jax
import jax.numpy as jnp
from jax import lax
from jax.sharding import PartitionSpec as P

ROUTE_SCALE = 2.5


def shards(tokens, expert_ids, gate_logits, w_gate, w_up, w_down):
    experts = lax.axis_size("expert")
    tok_count = tokens.shape[0]
    top_count = expert_ids.shape[1]
    model_width = tokens.shape[1]
    row_count = tok_count * top_count
    slot_total = 5 * row_count // 4
    capacity = slot_total // experts
    flat_ids = expert_ids.reshape(-1)
    onehot = (flat_ids[:, None] == jnp.arange(experts, dtype=jnp.int32)[None, :]).astype(jnp.int32)
    before = jnp.cumsum(onehot, axis=0) - onehot
    rank_col = jnp.sum(before * onehot, axis=1)
    slot_of = flat_ids * capacity + rank_col
    owner = jnp.arange(row_count, dtype=jnp.int32) // top_count
    placing = (slot_of[:, None] == jnp.arange(slot_total, dtype=jnp.int32)[None, :]).astype(
        jnp.bfloat16
    )
    picking = (owner[:, None] == jnp.arange(tok_count, dtype=jnp.int32)[None, :]).astype(
        jnp.bfloat16
    )
    select = jnp.einsum("rs,rt->st", placing, picking, preferred_element_type=jnp.float32).astype(
        jnp.bfloat16
    )
    outgoing = jnp.dot(select, tokens, preferred_element_type=jnp.float32).astype(jnp.bfloat16)
    outgoing = outgoing.reshape(experts, capacity, model_width)
    gate_half = w_gate[0]
    up_half = w_up[0]
    down_half = w_down[0]
    arrived = lax.all_to_all(outgoing, "expert", split_axis=0, concat_axis=0, tiled=True).reshape(
        slot_total, model_width
    )
    gate_pre = jnp.dot(
        arrived,
        lax.all_gather(gate_half, "zero", axis=0, tiled=True),
        preferred_element_type=jnp.float32,
    )
    up_pre = jnp.dot(
        arrived,
        lax.all_gather(up_half, "zero", axis=0, tiled=True),
        preferred_element_type=jnp.float32,
    )
    activated = (jax.nn.silu(gate_pre) * up_pre).astype(jnp.bfloat16)
    results = jnp.dot(
        activated,
        lax.all_gather(down_half, "zero", axis=1, tiled=True),
        preferred_element_type=jnp.float32,
    ).astype(jnp.bfloat16)
    returned = lax.all_to_all(
        results.reshape(experts, capacity, model_width),
        "expert",
        split_axis=0,
        concat_axis=0,
        tiled=True,
    )
    returned = returned.reshape(slot_total, model_width)
    scores = jax.nn.sigmoid(gate_logits)
    weights = ROUTE_SCALE * scores / jnp.sum(scores, axis=1, keepdims=True)
    gathered = returned[slot_of].reshape(tok_count, top_count, model_width)
    combined = jnp.sum(weights[:, :, None] * gathered.astype(jnp.float32), axis=1)
    return combined.astype(jnp.bfloat16)


def solution(mesh):
    return jax.shard_map(
        shards,
        mesh=mesh,
        in_specs=(
            P(("expert", "zero"), None),
            P(("expert", "zero"), None),
            P(("expert", "zero"), None),
            P("expert", "zero", None),
            P("expert", "zero", None),
            P("expert", None, "zero"),
        ),
        out_specs=P(("expert", "zero"), None),
        check_vma=False,
    )
```

profile of v0, /device:TPU:34, one launch (start us, length us, event | category | flops | bytes accessed | tf_op | source)
XLA Modules:
  0.0 672.5 jit_solution(3481544160874135072)
XLA Ops:
  6.5 0.0 copy-start
  6.5 0.0 all-gather.9.cloned.1.call-start
  6.5 0.7 all-gather.9.cloned.1.call-update
  7.3 0.0 all-gather.7.cloned.1.call-start
  7.3 0.7 all-gather.7.cloned.1.call-update
  8.0 0.0 copy-done.2
  8.0 0.1 copy.9
  8.1 0.1 eq.52
  8.2 0.1 reshape.83
  8.3 1.2 reduce-window.6
  9.5 0.2 slice_reduce_fusion
  9.8 0.1 fusion.18
  9.9 6.2 convolution_convert_fusion
  16.1 15.4 %reshape.85 = bf16[64,10,7168]{2,1,0:T(8,128)(2,1)} reshape(bf16[640,7168]{1,0:T(8,128)(2,1)} %convolution_convert_fusion) | data formatting | bytes 18350080 | tf_op jit(solution)/shard_map/reshape | solution.py:33
  31.5 11.3 %all-to-all-start = ((bf16[64,10,7168]{2,1,0:T(8,128)(2,1)}), bf16[64,10,7168]{2,1,0:T(8,128)(2,1)}, u32[]{:S(2)}, u32[]{:S(2)}) async-start(bf16[64,10,7168]{2,1,0:T(8,128)(2,1)} %reshape.85), calls=%async_computation | async-start | bytes 29360128 | tf_op jit(solution)/shard_map/all_to_all | solution.py:37
  42.8 0.2 all-gather.11.cloned.1.call-start
  43.0 0.5 all-gather.11.cloned.1.call-update
  43.5 257.2 %all-to-all-done = bf16[64,10,7168]{2,1,0:T(8,128)(2,1)} async-done(((bf16[64,10,7168]{2,1,0:T(8,128)(2,1)}), bf16[64,10,7168]{2,1,0:T(8,128)(2,1)}, u32[]{:S(2)}, u32[]{:S(2)}) %all-to-all-start) | async-done | bytes 9175072 | tf_op jit(solution)/shard_map/all_to_all | solution.py:37
  300.7 14.8 %reshape.86 = bf16[640,7168]{1,0:T(8,128)(2,1)} reshape(bf16[64,10,7168]{2,1,0:T(8,128)(2,1)} %all-to-all-done) | data formatting | bytes 18350080 | tf_op jit(solution)/shard_map/reshape | solution.py:37
  315.5 15.8 %fusion.3 = f32[640,1024]{1,0:T(8,128)} fusion(bf16[640,7168]{1,0:T(8,128)(2,1)} %reshape.86, bf16[1,7168,1024]{2,1,0:T(8,128)(2,1)} %all-gather.9.cloned.1.call-done), kind=kOutput, calls=%fused_computation.5 | convolution fusion | flops 9395240960 | bytes 26476544 | tf_op jit(solution)/shard_map/dot_general | solution.py:45
  331.3 16.4 %multiply_convert_fusion = bf16[640,1024]{1,0:T(8,128)(2,1)S(1)} fusion(f32[640,1024]{1,0:T(8,128)} %fusion.3, bf16[640,7168]{1,0:T(8,128)(2,1)} %reshape.86, bf16[1,7168,1024]{2,1,0:T(8,128)(2,1)} %all-gather.7.cloned.1.call-done), kind=kOutput, calls=%fused_computation.11 | convolution fusion | flops 9399173120 | bytes 27787264 | tf_op jit(solution)/shard_map/dot_general | solution.py:40
  347.7 0.0 all-gather.11.cloned.1.call-done
  347.7 17.0 %fusion.7 = bf16[640,7168]{1,0:T(8,128)(2,1)} fusion(bf16[640,1024]{1,0:T(8,128)(2,1)S(1)} %multiply_convert_fusion, bf16[1,1024,7168]{2,1,0:T(8,128)(2,1)} %all-gather.11.cloned.1.call-done), kind=kOutput, calls=%fused_computation.10 | convolution fusion | flops 9399828480 | bytes 25165824 | tf_op jit(solution)/shard_map/dot_general | solution.py:51
  364.7 14.5 %reshape.87 = bf16[64,10,7168]{2,1,0:T(8,128)(2,1)} reshape(bf16[640,7168]{1,0:T(8,128)(2,1)} %fusion.7) | data formatting | bytes 18350080 | tf_op jit(solution)/shard_map/reshape | solution.py:57
  379.2 8.0 %all-to-all-start.1 = ((bf16[64,10,7168]{2,1,0:T(8,128)(2,1)}), bf16[64,10,7168]{2,1,0:T(8,128)(2,1)}, u32[]{:S(2)}, u32[]{:S(2)}) async-start(bf16[64,10,7168]{2,1,0:T(8,128)(2,1)} %reshape.87), calls=%async_computation.1 | async-start | bytes 29360128 | tf_op jit(solution)/shard_map/all_to_all | solution.py:56
  387.3 0.1 copy.12
  387.4 0.1 mul.57
  387.5 0.1 copy.8
  387.6 235.1 %all-to-all-done.1 = bf16[64,10,7168]{2,1,0:T(8,128)(2,1)} async-done(((bf16[64,10,7168]{2,1,0:T(8,128)(2,1)}), bf16[64,10,7168]{2,1,0:T(8,128)(2,1)}, u32[]{:S(2)}, u32[]{:S(2)}) %all-to-all-start.1) | async-done | bytes 9175072 | tf_op jit(solution)/shard_map/all_to_all | solution.py:56
  622.7 14.8 %reshape.88 = bf16[640,7168]{1,0:T(8,128)(2,1)} reshape(bf16[64,10,7168]{2,1,0:T(8,128)(2,1)} %all-to-all-done.1) | data formatting | bytes 18350080 | tf_op jit(solution)/shard_map/reshape | solution.py:63
  637.5 18.7 %gather_fusion = bf16[512,7168]{1,0:T(8,128)(2,1)} fusion(bf16[640,7168]{1,0:T(8,128)(2,1)} %reshape.88, s32[1024]{0:T(1024)S(1)} %pad_clamp_fusion), kind=kCustom, calls=%fused_computation | custom fusion | bytes 14682112 | tf_op jit(solution)/shard_map/gather | solution.py:66
  656.2 9.8 %fusion = bf16[64,7168]{1,0:T(8,128)(2,1)} fusion(bf16[512,7168]{1,0:T(8,128)(2,1)} %gather_fusion, f32[64,8]{1,0:T(8,128)S(1)} %copy.8), kind=kLoop, calls=%fused_computation.2 | loop fusion | flops 10551296 | bytes 8259584 | tf_op jit(solution)/shard_map/reduce_sum | solution.py:67
  (17 shorter events, 0.1 us)
Async XLA Ops:
  6.5 3.4 copy-start
  6.5 1.5 copy-start.2
  6.5 309.0 %all-gather.9.cloned.1.call-start = ((), (), s32[]{:S(2)}) async-start(), calls=%async_computation.3 | async-start | bytes 22020096 | tf_op jit(solution)/shard_map/all_gather | solution.py:47
  7.3 324.0 %all-gather.7.cloned.1.call-start = ((), (), s32[]{:S(2)}) async-start(), calls=%async_computation.2 | async-start | bytes 22020096 | tf_op jit(solution)/shard_map/all_gather | solution.py:42
  31.5 269.2 %all-to-all-start = ((bf16[64,10,7168]{2,1,0:T(8,128)(2,1)}), bf16[64,10,7168]{2,1,0:T(8,128)(2,1)}, u32[]{:S(2)}, u32[]{:S(2)}) async-start(bf16[64,10,7168]{2,1,0:T(8,128)(2,1)} %reshape.85), calls=%async_computation | async-start | bytes 29360128 | tf_op jit(solution)/shard_map/all_to_all | solution.py:37
  42.8 304.9 %all-gather.11.cloned.1.call-start = ((), (), s32[]{:S(2)}) async-start(), calls=%async_computation.4 | async-start | bytes 22020096 | tf_op jit(solution)/shard_map/all_gather | solution.py:53
  379.2 8.2 %copy-start.3 = (f32[64,8]{0,1:T(8,128)S(1)}, f32[64,8]{0,1:T(8,128)}, u32[]{:S(2)}) copy-start(f32[64,8]{0,1:T(8,128)} %param.8) | copy-start | bytes 6148
  379.2 243.5 %all-to-all-start.1 = ((bf16[64,10,7168]{2,1,0:T(8,128)(2,1)}), bf16[64,10,7168]{2,1,0:T(8,128)(2,1)}, u32[]{:S(2)}, u32[]{:S(2)}) async-start(bf16[64,10,7168]{2,1,0:T(8,128)(2,1)} %reshape.87), calls=%async_computation.1 | async-start | bytes 29360128 | tf_op jit(solution)/shard_map/all_to_all | solution.py:56
  637.5 28.5 %copy-start.1 = (bf16[64,7168]{1,0:T(8,128)(2,1)S(1)}, bf16[64,7168]{1,0:T(8,128)(2,1)}, u32[]{:S(2)}) copy-start(bf16[64,7168]{1,0:T(8,128)(2,1)} %param.6) | copy-start | bytes 2752516
Sparse Core Ops, SparseCore 0:
  9.0 31.7 all-gather.8
  42.5 31.0 all-gather.6
  75.3 31.0 all-gather.10
where the time goes:
time: 674 us; the launch traced here: 673 us
  waiting for transfers between devices  494 us (73%)
  local copies, waits for them, and re-layouts  78.9 us (12%)
  matrix products  55.4 us (8%)
  starting transfers between devices  19.6 us (3%)
  between operations  13.2 us (2%)
  other arithmetic  11.3 us (2%)
    all_to_all x1, waiting for transfers between devices, shards(): lax.all_to_all(outgoing, 'expert', split_axis=0, concat_axis=0, tiled=True)  257 us
    all_to_all x1, waiting for transfers between devices, shards(): lax.all_to_all(results.reshape(experts, capacity, model_width), 'expert',...  235 us
    gather x1, local copies, waits for them, and re-layouts, shards(): gathered = returned[slot_of].reshape(tok_count, top_count, model_width)  18.7 us
    dot_general x1, matrix products, shards(): jnp.dot(activated, lax.all_gather(down_half, 'zero', axis=1, tiled=True),...  17 us
    dot_general x1, matrix products, shards(): jnp.dot(arrived, lax.all_gather(gate_half, 'zero', axis=0, tiled=True), p...  16.4 us
    dot_general x1, matrix products, shards(): jnp.dot(arrived, lax.all_gather(up_half, 'zero', axis=0, tiled=True), pre...  15.8 us
    reshape x1, local copies, waits for them, and re-layouts, shards(): outgoing = outgoing.reshape(experts, capacity, model_width)  15.4 us
    reshape x1, local copies, waits for them, and re-layouts, shards(): lax.all_to_all(outgoing, 'expert', split_axis=0, concat_axis=0, tiled=True)  14.8 us
  transfers between devices with their start and end apart: 5, of which 2 were waited for; matrix products, arithmetic and copies ran while one was open for 11% of the time, Pallas kernels for 0%

commit v1 on v0

v1 whole, which is shorter than its diff:
```python
import jax
import jax.numpy as jnp
from jax import lax
from jax.experimental import pallas as pl
from jax.experimental.pallas import tpu as pltpu
from jax.sharding import PartitionSpec as P

ROUTE_SCALE = 2.5
MAIN = 8
REST = 2
FOLD = MAIN // REST
F32, BF16 = jnp.float32, jnp.bfloat16


def slot_table(ids_ref, experts, tok_count):
    row = lax.broadcasted_iota(jnp.int32, (experts, tok_count), 0)
    chosen = jnp.zeros((experts, tok_count), F32)
    for k in range(ids_ref.shape[0]):
        chosen = chosen + jnp.where(ids_ref[k : k + 1, :] == row, 1.0, 0.0)
    earlier = (
        lax.broadcasted_iota(jnp.int32, (tok_count, tok_count), 0)
        < lax.broadcasted_iota(jnp.int32, (tok_count, tok_count), 1)
    ).astype(F32)
    rank = jnp.dot(chosen.astype(BF16), earlier.astype(BF16), preferred_element_type=F32)
    slot = jnp.where(chosen > 0, rank, -1.0)
    return jnp.broadcast_to(slot[:, None, :], (experts, MAIN, tok_count)).reshape(experts * MAIN, tok_count)


def slot_masks(slot):
    sub = lax.broadcasted_iota(jnp.int32, slot.shape, 0) % MAIN
    main = slot == sub.astype(F32)
    rest = slot == (MAIN + sub % REST).astype(F32)
    return main, [rest & (sub // REST == j) for j in range(FOLD)]


def pack_body(ids_ref, tok_ref, out_ref, sel_ref, *, experts):
    step = pl.program_id(0)
    width = out_ref.shape[1]
    tok_count = tok_ref.shape[0]

    @pl.when(step == 0)
    def _():
        main, rest = slot_masks(slot_table(ids_ref, experts, tok_count))
        for n, mask in enumerate([main] + rest):
            sel_ref[n] = jnp.where(mask, 1.0, 0.0).astype(BF16)

    @pl.when(step < FOLD)
    def _():
        cols = tok_ref[:, pl.ds(pl.multiple_of(step * width, 128), width)]
        out_ref[...] = jnp.dot(sel_ref[0], cols, preferred_element_type=F32).astype(BF16)

    @pl.when(step == FOLD)
    def _():
        total = jnp.dot(sel_ref[1], tok_ref[:, :width], preferred_element_type=F32)
        for j in range(1, FOLD):
            total += jnp.dot(sel_ref[1 + j], tok_ref[:, j * width : (j + 1) * width], preferred_element_type=F32)
        out_ref[...] = total.astype(BF16)


def pack(ids_t, tokens, experts):
    tok_count, model = tokens.shape
    width = model // FOLD
    rows = experts * MAIN
    return pl.pallas_call(
        lambda *refs: pack_body(*refs, experts=experts),
        grid=(FOLD + 1,),
        in_specs=[
            pl.BlockSpec(ids_t.shape, lambda i: (0, 0)),
            pl.BlockSpec(tokens.shape, lambda i: (0, 0)),
        ],
        out_specs=pl.BlockSpec((rows, width), lambda i: (0, i)),
        out_shape=jax.ShapeDtypeStruct((rows, model + width), BF16),
        scratch_shapes=[pltpu.VMEM((1 + FOLD, rows, tok_count), BF16)],
        name="pack_rows",
    )(ids_t, tokens)


def folding(rows, j):
    count = rows // FOLD
    whole = lax.broadcasted_iota(jnp.int32, (count, rows), 0)
    folded = lax.broadcasted_iota(jnp.int32, (count, rows), 1)
    target = (whole // REST) * MAIN + j * REST + whole % REST
    return jnp.where(folded == target, 1.0, 0.0).astype(BF16)


def ffn_body(x_ref, left_ref, wg_ref, wu_ref, wd_ref, out_ref, gate_ref, up_ref, act_ref, fold_ref, *, parts):
    step = pl.program_id(0)
    rows = x_ref.shape[0]
    width = x_ref.shape[1]
    k_steps = FOLD * parts

    @pl.when(step < k_steps)
    def _():
        j, h = step // parts, step % parts
        left = left_ref[:, pl.ds(pl.multiple_of(h * width, 128), width)]
        extra = jnp.dot(folding(rows, j), left, preferred_element_type=F32).astype(BF16)
        x = jnp.concatenate([x_ref[...], extra], axis=0)
        gate = jnp.dot(x, wg_ref[...], preferred_element_type=F32)
        up = jnp.dot(x, wu_ref[...], preferred_element_type=F32)

        @pl.when(step == 0)
        def _():
            gate_ref[...] = gate
            up_ref[...] = up

        @pl.when(step > 0)
        def _():
            gate_ref[...] += gate
            up_ref[...] += up

    @pl.when(step == k_steps)
    def _():
        gate = gate_ref[...]
        act_ref[...] = ((gate / (1.0 + jnp.exp(-gate))) * up_ref[...]).astype(BF16)
        fold_ref[...] = jnp.zeros(fold_ref.shape, BF16)

    @pl.when((step >= k_steps) & (step < 2 * k_steps))
    def _():
        j, h = (step - k_steps) // parts, (step - k_steps) % parts
        y = jnp.dot(act_ref[...], wd_ref[...], preferred_element_type=F32).astype(BF16)
        out_ref[...] = y[:rows]
        back = lax.dot_general(
            folding(rows, j), y[rows:], (((0,), (0,)), ((), ())), preferred_element_type=F32
        ).astype(BF16)
        cols = pl.ds(pl.multiple_of(h * width, 128), width)
        fold_ref[:, cols] = fold_ref[:, cols] + back

    @pl.when(step >= 2 * k_steps)
    def _():
        h = step - 2 * k_steps
        out_ref[...] = fold_ref[:, pl.ds(pl.multiple_of(h * width, 128), width)]


def ffn(x, w_gate, w_up, w_down, parts=2):
    rows, total = x.shape
    model, hidden = w_gate.shape
    fold_width = model // FOLD
    width = fold_width // parts
    k_steps = FOLD * parts
    all_rows = rows + rows // FOLD
    return pl.pallas_call(
        lambda *refs: ffn_body(*refs, parts=parts),
        grid=(2 * k_steps + parts,),
        in_specs=[
            pl.BlockSpec((rows, width), lambda i: (0, jnp.minimum(i, k_steps - 1))),
            pl.BlockSpec((rows, fold_width), lambda i: (0, FOLD)),
            pl.BlockSpec((width, hidden), lambda i: (jnp.minimum(i, k_steps - 1), 0)),
            pl.BlockSpec((width, hidden), lambda i: (jnp.minimum(i, k_steps - 1), 0)),
            pl.BlockSpec((hidden, width), lambda i: (0, jnp.clip(i - k_steps, 0, k_steps - 1))),
        ],
        out_specs=pl.BlockSpec((rows, width), lambda i: (0, jnp.maximum(i - k_steps, 0))),
        out_shape=jax.ShapeDtypeStruct((rows, total), BF16),
        scratch_shapes=[
            pltpu.VMEM((all_rows, hidden), F32),
            pltpu.VMEM((all_rows, hidden), F32),
            pltpu.VMEM((all_rows, hidden), BF16),
            pltpu.VMEM((rows, fold_width), BF16),
        ],
        compiler_params=pltpu.CompilerParams(vmem_limit_bytes=56 * 1024 * 1024),
        name="expert_ffn",
    )(x, x, w_gate, w_up, w_down)


def merge_body(ids_ref, logit_ref, y_ref, left_ref, out_ref, mix_ref, *, experts):
    step = pl.program_id(0)
    tok_count = out_ref.shape[0]

    @pl.when(step == 0)
    def _():
        scores = 1.0 / (1.0 + jnp.exp(-logit_ref[...]))
        weights = ROUTE_SCALE * scores / jnp.sum(scores, axis=0, keepdims=True)
        row = lax.broadcasted_iota(jnp.int32, (experts, tok_count), 0)
        gain = jnp.zeros((experts, tok_count), F32)
        for k in range(ids_ref.shape[0]):
            gain = gain + jnp.where(ids_ref[k : k + 1, :] == row, weights[k : k + 1, :], 0.0)
        gain = jnp.broadcast_to(gain[:, None, :], (experts, MAIN, tok_count)).reshape(experts * MAIN, tok_count)
        main, rest = slot_masks(slot_table(ids_ref, experts, tok_count))
        for n, mask in enumerate([main] + rest):
            part = jnp.where(mask, gain, 0.0)
            high = part.astype(BF16).astype(F32)
            both = jnp.concatenate([high, part - high], axis=1)
            mix_ref[n] = both.T.astype(BF16)

    total = jnp.dot(mix_ref[0], y_ref[...], preferred_element_type=F32)
    total += jnp.dot(mix_ref[1 + step], left_ref[...], preferred_element_type=F32)
    out_ref[...] = (total[:tok_count] + total[tok_count:]).astype(BF16)


def merge(ids_t, logits_t, y, experts):
    tok_count = ids_t.shape[1]
    rows, total = y.shape
    width = total // (FOLD + 1)
    return pl.pallas_call(
        lambda *refs: merge_body(*refs, experts=experts),
        grid=(FOLD,),
        in_specs=[
            pl.BlockSpec(ids_t.shape, lambda i: (0, 0)),
            pl.BlockSpec(logits_t.shape, lambda i: (0, 0)),
            pl.BlockSpec((rows, width), lambda i: (0, i)),
            pl.BlockSpec((rows, width), lambda i: (0, FOLD)),
        ],
        out_specs=pl.BlockSpec((tok_count, width), lambda i: (0, i)),
        out_shape=jax.ShapeDtypeStruct((tok_count, width * FOLD), BF16),
        scratch_shapes=[pltpu.VMEM((1 + FOLD, 2 * tok_count, rows), BF16)],
        name="merge_rows",
    )(ids_t, logits_t, y, y)


def exchange(x, experts):
    rows, total = x.shape
    out = lax.all_to_all(x.reshape(experts, rows // experts, total), "expert", split_axis=0, concat_axis=0, tiled=True)
    return out.reshape(rows, total)


def shards(tokens, expert_ids, gate_logits, w_gate, w_up, w_down):
    experts = lax.axis_size("expert")
    ids_t, logits_t = expert_ids.T, gate_logits.T
    gate_full = lax.all_gather(w_gate[0], "zero", axis=0, tiled=True)
    up_full = lax.all_gather(w_up[0], "zero", axis=0, tiled=True)
    down_full = lax.all_gather(w_down[0], "zero", axis=1, tiled=True)
    arrived = exchange(pack(ids_t, tokens, experts), experts)
    results = ffn(arrived, gate_full, up_full, down_full)
    return merge(ids_t, logits_t, exchange(results, experts), experts)


def solution(mesh):
    return jax.shard_map(
        shards,
        mesh=mesh,
        in_specs=(
            P(("expert", "zero"), None),
            P(("expert", "zero"), None),
            P(("expert", "zero"), None),
            P("expert", "zero", None),
            P("expert", "zero", None),
            P("expert", None, "zero"),
        ),
        out_specs=P(("expert", "zero"), None),
        check_vma=False,
    )
```

time: 674 us -> 311 us (0.46)
  waiting for transfers between devices: 494 us -> 2.09 us
  blocking collectives: 0 us -> 226 us
  local copies, waits for them, and re-layouts: 78.9 us -> 0 us
  Pallas kernels: 0 us -> 66.4 us
  matrix products: 55.4 us -> 0 us
  starting transfers between devices: 19.6 us -> 0.08 us
  other arithmetic: 11.3 us -> 0 us
    all_to_all x2 -> x0, waiting for transfers between devices: 492 us -> none  [the longest x1 257 us: shards(): lax.all_to_all(outgoing, 'expert', split_axis=0, concat_axis=0, tiled=True)]
    all_to_all x0 -> x2, blocking collectives: none -> 226 us  [exchange(): lax.all_to_all(x.reshape(experts, rows // experts, total), 'expert', spli...]
    pallas_call x0 -> x3, Pallas kernels: none -> 66.4 us  [the longest x1 50 us: ffn(): pl.pallas_call(lambda *refs: ffn_body(*refs, parts=parts), grid=(2 * k_st...]
    reshape x5 -> x0, local copies, waits for them, and re-layouts: 59.6 us -> none  [the longest x1 15.4 us: shards(): outgoing = outgoing.reshape(experts, capacity, model_width)]
    dot_general x4 -> x0, matrix products: 55.4 us -> none  [the longest x1 17 us: shards(): jnp.dot(activated, lax.all_gather(down_half, 'zero', axis=1, tiled=True),...]
    all_to_all x2 -> x0, starting transfers between devices: 19.3 us -> none  [the longest x1 11.3 us: shards(): lax.all_to_all(outgoing, 'expert', split_axis=0, concat_axis=0, tiled=True)]
    gather x1 -> x0, local copies, waits for them, and re-layouts: 18.7 us -> none  [shards(): gathered = returned[slot_of].reshape(tok_count, top_count, model_width)]
    reduce_sum x3 -> x0, other arithmetic: 9.98 us -> none  [the longest x1 9.83 us: shards(): jnp.sum(weights[:, :, None] * gathered.astype(jnp.float32), axis=1)]
  transfers between devices with their start and end apart: 5 -> 3, of which waited for: 2 -> 0; matrix products, arithmetic and copies ran while one was open for 11% -> 0% of each run, Pallas kernels for 0% -> 3%
where the time goes in v1:
time: 311 us; the launch traced here: 308 us
  blocking collectives  226 us (73%)
  Pallas kernels  66.4 us (21%)
  between operations  13.1 us (4%)
    all_to_all x2, blocking collectives, exchange(): lax.all_to_all(x.reshape(experts, rows // experts, total), 'expert', spli...  226 us
    pallas_call x1, Pallas kernels, ffn(): pl.pallas_call(lambda *refs: ffn_body(*refs, parts=parts), grid=(2 * k_st...  50 us
    pallas_call x1, Pallas kernels, pack(): pl.pallas_call(lambda *refs: pack_body(*refs, experts=experts), grid=(FOL...  9.04 us
    pallas_call x1, Pallas kernels, merge(): pl.pallas_call(lambda *refs: merge_body(*refs, experts=experts), grid=(FO...  7.38 us
  transfers between devices with their start and end apart: 3, of which 0 were waited for; matrix products, arithmetic and copies ran while one was open for 0% of the time, Pallas kernels for 3%

profile of v1, /device:TPU:34, one launch (start us, length us, event | category | flops | bytes accessed | tf_op | source)
XLA Modules:
  0.0 307.9 jit_solution(12911424701171919186)
XLA Ops:
  6.5 0.0 all-gather.7.cloned.1.call-start
  6.5 0.7 all-gather.7.cloned.1.call-update
  7.3 0.0 all-gather.9.cloned.1.call-start
  7.3 0.7 all-gather.9.cloned.1.call-update
  8.0 0.0 all-gather.11.cloned.1.call-start
  8.1 0.7 all-gather.11.cloned.1.call-update
  8.7 9.0 %pack_rows.1 = bf16[512,8960]{1,0:T(8,128)(2,1)} custom-call(s32[8,64]{1,0:T(8,128)} %bitcast.18, bf16[64,7168]{1,0:T(8,128)(2,1)} %refs_1_.1), custom_call_target="tpu_custom_call" | custom-call | tf_op jit(solution)/shard_map/pack_rows/pallas_call | solution.py:64
  17.8 115.7 %all_to_all.10 = bf16[64,8,8960]{2,1,0:T(8,128)(2,1)} all-to-all(bf16[64,8,8960]{2,1,0:T(8,128)(2,1)} %bitcast.14), channel_id=1, replica_groups=mesh['expert'=64,'zero'=2] {'expert'}, dimensions={0} | all-to-all | bytes 18350080 | tf_op jit(solution)/shard_map/all_to_all | solution.py:211
  133.5 0.0 all-gather.7.cloned.1.call-done
  133.5 0.0 all-gather.9.cloned.1.call-done
  133.5 0.0 all-gather.11.cloned.1.call-done
  133.5 50.0 %expert_ffn.1 = bf16[512,8960]{1,0:T(8,128)(2,1)} custom-call(bf16[512,8960]{1,0:T(8,128)(2,1)} %bitcast.9, bf16[512,8960]{1,0:T(8,128)(2,1)} %bitcast.10, bf16[7168,1024]{1,0:T(8,128)(2,1)} %bitcast.15, bf16[7168,1024]{1,0:T(8,128)(2,1)} %bitcast.16, bf16[1024,7168]{1,0:T(8,128)(2,1)} %bitcast.17), custom_call_target="tpu_custom_call" | custom-call | tf_op jit(solution)/shard_map/expert_ffn/pallas_call | solution.py:141
  183.5 110.5 %all_to_all.11 = bf16[64,8,8960]{2,1,0:T(8,128)(2,1)} all-to-all(bf16[64,8,8960]{2,1,0:T(8,128)(2,1)} %bitcast.13), channel_id=1, replica_groups=mesh['expert'=64,'zero'=2] {'expert'}, dimensions={0} | all-to-all | bytes 18350080 | tf_op jit(solution)/shard_map/all_to_all | solution.py:211
  294.0 7.4 %merge_rows.1 = bf16[64,7168]{1,0:T(8,128)(2,1)} custom-call(s32[8,64]{1,0:T(8,128)} %bitcast.19, f32[8,64]{1,0:T(8,128)} %bitcast.20, bf16[512,8960]{1,0:T(8,128)(2,1)} %bitcast.11, bf16[512,8960]{1,0:T(8,128)(2,1)} %bitcast.12), custom_call_target="tpu_custom_call" | custom-call | tf_op jit(solution)/shard_map/merge_rows/pallas_call | solution.py:193
Async XLA Ops:
  6.5 127.0 %all-gather.7.cloned.1.call-start = ((), (), s32[]{:S(2)}) async-start(), calls=%async_computation.2 | async-start | bytes 22020096 | tf_op jit(solution)/shard_map/all_gather | solution.py:218
  7.3 126.3 %all-gather.9.cloned.1.call-start = ((), (), s32[]{:S(2)}) async-start(), calls=%async_computation.3 | async-start | bytes 22020096 | tf_op jit(solution)/shard_map/all_gather | solution.py:219
  8.0 125.5 %all-gather.11.cloned.1.call-start = ((), (), s32[]{:S(2)}) async-start(), calls=%async_computation.4 | async-start | bytes 22020096 | tf_op jit(solution)/shard_map/all_gather | solution.py:220
Sparse Core Ops, SparseCore 0:
  9.0 31.7 all-gather.6
  42.5 31.0 all-gather.8
  75.3 31.0 all-gather.10

commit v2 on v1

--- a/solution.py
+++ b/solution.py
@@ -4,6 +4,7 @@
 from jax.experimental import pallas as pl
 from jax.experimental.pallas import tpu as pltpu
 from jax.sharding import PartitionSpec as P
+
 
 ROUTE_SCALE = 2.5
 MAIN = 8
@@ -33,7 +34,7 @@
     return main, [rest & (sub // REST == j) for j in range(FOLD)]
 
 
-def pack_body(ids_ref, tok_ref, out_ref, sel_ref, *, experts):
+def pack_body(ids_ref, tok_ref, out_ref, sel_ref, all_ref, *, experts):
     step = pl.program_id(0)
     width = out_ref.shape[1]
     tok_count = tok_ref.shape[0]
@@ -41,20 +42,18 @@
     @pl.when(step == 0)
     def _():
         main, rest = slot_masks(slot_table(ids_ref, experts, tok_count))
-        for n, mask in enumerate([main] + rest):
-            sel_ref[n] = jnp.where(mask, 1.0, 0.0).astype(BF16)
+        sel_ref[...] = jnp.where(main, 1.0, 0.0).astype(BF16)
+        all_ref[...] = jnp.concatenate([jnp.where(mask, 1.0, 0.0) for mask in rest], axis=1).astype(BF16)
 
     @pl.when(step < FOLD)
     def _():
         cols = tok_ref[:, pl.ds(pl.multiple_of(step * width, 128), width)]
-        out_ref[...] = jnp.dot(sel_ref[0], cols, preferred_element_type=F32).astype(BF16)
+        out_ref[...] = jnp.dot(sel_ref[...], cols, preferred_element_type=F32).astype(BF16)
 
     @pl.when(step == FOLD)
     def _():
-        total = jnp.dot(sel_ref[1], tok_ref[:, :width], preferred_element_type=F32)
-        for j in range(1, FOLD):
-            total += jnp.dot(sel_ref[1 + j], tok_ref[:, j * width : (j + 1) * width], preferred_element_type=F32)
-        out_ref[...] = total.astype(BF16)
+        stack = jnp.concatenate([tok_ref[:, j * width : (j + 1) * width] for j in range(FOLD)], axis=0)
+        out_ref[...] = jnp.dot(all_ref[...], stack, preferred_element_type=F32).astype(BF16)
 
 
 def pack(ids_t, tokens, experts):
@@ -70,7 +69,7 @@
         ],
         out_specs=pl.BlockSpec((rows, width), lambda i: (0, i)),
         out_shape=jax.ShapeDtypeStruct((rows, model + width), BF16),
-        scratch_shapes=[pltpu.VMEM((1 + FOLD, rows, tok_count), BF16)],
+        scratch_shapes=[pltpu.VMEM((rows, tok_count), BF16), pltpu.VMEM((rows, FOLD * tok_count), BF16)],
         name="pack_rows",
     )(ids_t, tokens)
 
@@ -83,82 +82,135 @@
     return jnp.where(folded == target, 1.0, 0.0).astype(BF16)
 
 
-def ffn_body(x_ref, left_ref, wg_ref, wu_ref, wd_ref, out_ref, gate_ref, up_ref, act_ref, fold_ref, *, parts):
+def ffn_body(z_ref, x_ref, left_ref, g0, g1, u0, u1, d0, d1, out_ref, gate_ref, up_ref, act_ref, fold_ref, in_ref, down_ref, in_sem, down_sem):
     step = pl.program_id(0)
-    rows = x_ref.shape[0]
-    width = x_ref.shape[1]
-    k_steps = FOLD * parts
-
-    @pl.when(step < k_steps)
-    def _():
-        j, h = step // parts, step % parts
-        left = left_ref[:, pl.ds(pl.multiple_of(h * width, 128), width)]
-        extra = jnp.dot(folding(rows, j), left, preferred_element_type=F32).astype(BF16)
+    rows, width = x_ref.shape
+    half = FOLD // 2
+    cut = (width // 512) * 256
+    pieces = ((0, cut), (cut, width - cut))
+    z = z_ref[0]
+
+    def project_copies(source, first, slot):
+        return [
+            pltpu.make_async_copy(
+                source[n].at[pl.ds(first + at, size)], in_ref.at[slot, n, pl.ds(at, size)], in_sem.at[slot, n, p]
+            )
+            for p, (at, size) in enumerate(pieces)
+            for n in range(2)
+        ]
+
+    def expand_copy(source, first, slot):
+        return pltpu.make_async_copy(source.at[:, pl.ds(first, width)], down_ref.at[slot], down_sem.at[slot])
+
+    def start(block):
+        if block < FOLD:
+            source = (g0, u0) if block < half else (g1, u1)
+            for copy in project_copies(source, (block % half) * width, block % 2):
+                copy.start()
+        else:
+            source = d0 if block - FOLD < half else d1
+            expand_copy(source, (block % half) * width, block % 2).start()
+
+    @pl.when(step == 0)
+    def _():
+        start(0)
+
+    for block in range(1, 2 * FOLD):
+        @pl.when(step == block - 1)
+        def _(block=block):
+            start(block)
+
+    slot = step % 2
+
+    def place_of(i):
+        return jnp.where(i < half, z * half + i, (1 - z) * half + i - half)
+
+    @pl.when(step < FOLD)
+    def _():
+        extra = jnp.dot(folding(rows, place_of(step)), left_ref[...], preferred_element_type=F32).astype(BF16)
         x = jnp.concatenate([x_ref[...], extra], axis=0)
-        gate = jnp.dot(x, wg_ref[...], preferred_element_type=F32)
-        up = jnp.dot(x, wu_ref[...], preferred_element_type=F32)
+        copies = project_copies((g0, u0), 0, slot)
+        total = [None, None]
+        for p, (at, size) in enumerate(pieces):
+            for n in range(2):
+                copies[2 * p + n].wait()
+            for n in range(2):
+                part = jnp.dot(x[:, at : at + size], in_ref[slot, n, at : at + size], preferred_element_type=F32)
+                total[n] = part if p == 0 else total[n] + part
 
         @pl.when(step == 0)
         def _():
-            gate_ref[...] = gate
-            up_ref[...] = up
+            gate_ref[...] = total[0]
+            up_ref[...] = total[1]
 
         @pl.when(step > 0)
         def _():
-            gate_ref[...] += gate
-            up_ref[...] += up
-
-    @pl.when(step == k_steps)
+            gate_ref[...] += total[0]
+            up_ref[...] += total[1]
+
+    @pl.when(step == FOLD)
     def _():
         gate = gate_ref[...]
         act_ref[...] = ((gate / (1.0 + jnp.exp(-gate))) * up_ref[...]).astype(BF16)
         fold_ref[...] = jnp.zeros(fold_ref.shape, BF16)
 
-    @pl.when((step >= k_steps) & (step < 2 * k_steps))
-    def _():
-        j, h = (step - k_steps) // parts, (step - k_steps) % parts
-        y = jnp.dot(act_ref[...], wd_ref[...], preferred_element_type=F32).astype(BF16)
+    @pl.when((step >= FOLD) & (step < 2 * FOLD))
+    def _():
+        expand_copy(d0, 0, slot).wait()
+        y = jnp.dot(act_ref[...], down_ref[slot], preferred_element_type=F32).astype(BF16)
         out_ref[...] = y[:rows]
         back = lax.dot_general(
-            folding(rows, j), y[rows:], (((0,), (0,)), ((), ())), preferred_element_type=F32
-        ).astype(BF16)
-        cols = pl.ds(pl.multiple_of(h * width, 128), width)
-        fold_ref[:, cols] = fold_ref[:, cols] + back
-
-    @pl.when(step >= 2 * k_steps)
-    def _():
-        h = step - 2 * k_steps
-        out_ref[...] = fold_ref[:, pl.ds(pl.multiple_of(h * width, 128), width)]
-
-
-def ffn(x, w_gate, w_up, w_down, parts=2):
+            folding(rows, place_of(step - FOLD)), y[rows:], (((0,), (0,)), ((), ())), preferred_element_type=F32
+        )
+        fold_ref[...] += back.astype(BF16)
+
+    @pl.when(step == 2 * FOLD)
+    def _():
+        out_ref[...] = fold_ref[...]
+
+
+def ffn(place, x, weights):
     rows, total = x.shape
-    model, hidden = w_gate.shape
-    fold_width = model // FOLD
-    width = fold_width // parts
-    k_steps = FOLD * parts
+    (g0, g1), (u0, u1), (d0, d1) = weights
+    hidden = g0.shape[1]
+    half = FOLD // 2
+    width = g0.shape[0] // half
     all_rows = rows + rows // FOLD
+
+    def place_of(i, z_ref):
+        z = z_ref[0]
+        return jnp.where(i < half, z * half + i, (1 - z) * half + i - half)
+
+    def out_place(i, z_ref):
+        return jnp.where(i >= 2 * FOLD, FOLD, place_of(jnp.clip(i - FOLD, 0, FOLD - 1), z_ref))
+
+    whole = pl.BlockSpec(memory_space=pl.ANY)
     return pl.pallas_call(
-        lambda *refs: ffn_body(*refs, parts=parts),
-        grid=(2 * k_steps + parts,),
-        in_specs=[
-            pl.BlockSpec((rows, width), lambda i: (0, jnp.minimum(i, k_steps - 1))),
-            pl.BlockSpec((rows, fold_width), lambda i: (0, FOLD)),
-            pl.BlockSpec((width, hidden), lambda i: (jnp.minimum(i, k_steps - 1), 0)),
-            pl.BlockSpec((width, hidden), lambda i: (jnp.minimum(i, k_steps - 1), 0)),
-            pl.BlockSpec((hidden, width), lambda i: (0, jnp.clip(i - k_steps, 0, k_steps - 1))),
-        ],
-        out_specs=pl.BlockSpec((rows, width), lambda i: (0, jnp.maximum(i - k_steps, 0))),
+        ffn_body,
+        grid_spec=pltpu.PrefetchScalarGridSpec(
+            num_scalar_prefetch=1,
+            grid=(2 * FOLD + 1,),
+            in_specs=[
+                pl.BlockSpec((rows, width), lambda i, z_ref: (0, place_of(jnp.minimum(i, FOLD - 1), z_ref))),
+                pl.BlockSpec((rows, width), lambda i, z_ref: (0, FOLD)),
+                *[whole] * 6,
+            ],
+            out_specs=pl.BlockSpec((rows, width), lambda i, z_ref: (0, out_place(i, z_ref))),
+            scratch_shapes=[
+                pltpu.VMEM((all_rows, hidden), F32),
+                pltpu.VMEM((all_rows, hidden), F32),
+                pltpu.VMEM((all_rows, hidden), BF16),
+                pltpu.VMEM((rows, width), BF16),
+                pltpu.VMEM((2, 2, width, hidden), BF16),
+                pltpu.VMEM((2, hidden, width), BF16),
+                pltpu.SemaphoreType.DMA((2, 2, 2)),
+                pltpu.SemaphoreType.DMA((2,)),
+            ],
+        ),
         out_shape=jax.ShapeDtypeStruct((rows, total), BF16),
-        scratch_shapes=[
-            pltpu.VMEM((all_rows, hidden), F32),
-            pltpu.VMEM((all_rows, hidden), F32),
-            pltpu.VMEM((all_rows, hidden), BF16),
-            pltpu.VMEM((rows, fold_width), BF16),
-        ],
-        compiler_params=pltpu.CompilerParams(vmem_limit_bytes=56 * 1024 * 1024),
+        compiler_params=pltpu.CompilerParams(vmem_limit_bytes=58 * 1024 * 1024),
         name="expert_ffn",
-    )(x, x, w_gate, w_up, w_down)
+    )(place, x, x, g0, g1, u0, u1, d0, d1)
 
 
 def merge_body(ids_ref, logit_ref, y_ref, left_ref, out_ref, mix_ref, *, experts):
@@ -214,13 +266,18 @@
 
 def shards(tokens, expert_ids, gate_logits, w_gate, w_up, w_down):
     experts = lax.axis_size("expert")
+    place = lax.axis_index("zero").astype(jnp.int32).reshape(1)
+    place, tokens = lax.optimization_barrier((place, tokens))
     ids_t, logits_t = expert_ids.T, gate_logits.T
-    gate_full = lax.all_gather(w_gate[0], "zero", axis=0, tiled=True)
-    up_full = lax.all_gather(w_up[0], "zero", axis=0, tiled=True)
-    down_full = lax.all_gather(w_down[0], "zero", axis=1, tiled=True)
-    arrived = exchange(pack(ids_t, tokens, experts), experts)
-    results = ffn(arrived, gate_full, up_full, down_full)
-    return merge(ids_t, logits_t, exchange(results, experts), experts)
+    swap = [(0, 1), (1, 0)]
+    weights = []
+    for w in (w_gate, w_up, w_down):
+        weights.append((w[0], lax.ppermute(w[0], "zero", swap)))
+    packed = pack(ids_t, tokens, experts)
+    arrived = exchange(packed, experts)
+    results = ffn(place, arrived, weights)
+    returned = exchange(results, experts)
+    return merge(ids_t, logits_t, returned, experts)
 
 
 def solution(mesh):

time: 311 us -> 314 us (level)
  waiting for transfers between devices: 2.09 us -> 131 us
  blocking collectives: 226 us -> 109 us
  between operations: 13.1 us -> 0.03 us
  starting transfers between devices: 0.08 us -> 11.9 us
  Pallas kernels: 66.4 us -> 59.5 us
    all_to_all x2 -> x1, blocking collectives: 226 us -> 109 us  [exchange(): lax.all_to_all(x.reshape(experts, rows // experts, total), 'expert', spli...]
    all_to_all x0 -> x1, waiting for transfers between devices: none -> 98.1 us  [exchange(): lax.all_to_all(x.reshape(experts, rows // experts, total), 'expert', spli...]
    ppermute x0 -> x3, waiting for transfers between devices: none -> 32.4 us  [shards(): weights.append((w[0], lax.ppermute(w[0], 'zero', swap)))]
    all_to_all x0 -> x1, starting transfers between devices: none -> 11.2 us  [exchange(): lax.all_to_all(x.reshape(experts, rows // experts, total), 'expert', spli...]
    pallas_call x1, Pallas kernels: 50 us -> 44.7 us  [ffn(): pl.pallas_call(ffn_body, grid_spec=pltpu.PrefetchScalarGridSpec(num_scala...]
  transfers between devices with their start and end apart: 3 -> 4, of which waited for: 0 -> 4; matrix products, arithmetic and copies ran while one was open for 0% -> 0% of each run, Pallas kernels for 3% -> 0%
where the time goes in v2:
time: 314 us; the launch traced here: 311 us
  waiting for transfers between devices  131 us (42%)
  blocking collectives  109 us (35%)
  Pallas kernels  59.5 us (19%)
  starting transfers between devices  11.9 us (4%)
    all_to_all x1, blocking collectives, exchange(): lax.all_to_all(x.reshape(experts, rows // experts, total), 'expert', spli...  109 us
    all_to_all x1, waiting for transfers between devices, exchange(): lax.all_to_all(x.reshape(experts, rows // experts, total), 'expert', spli...  98.1 us
    pallas_call x1, Pallas kernels, ffn(): pl.pallas_call(ffn_body, grid_spec=pltpu.PrefetchScalarGridSpec(num_scala...  44.7 us
    ppermute x3, waiting for transfers between devices, shards(): weights.append((w[0], lax.ppermute(w[0], 'zero', swap)))  32.4 us
    all_to_all x1, starting transfers between devices, exchange(): lax.all_to_all(x.reshape(experts, rows // experts, total), 'expert', spli...  11.2 us
    pallas_call x1, Pallas kernels, pack(): pl.pallas_call(lambda *refs: pack_body(*refs, experts=experts), grid=(FOL...  7.43 us
    pallas_call x1, Pallas kernels, merge(): pl.pallas_call(lambda *refs: merge_body(*refs, experts=experts), grid=(FO...  7.38 us
  transfers between devices with their start and end apart: 4, of which 4 were waited for; matrix products, arithmetic and copies ran while one was open for 0% of the time, Pallas kernels for 0%

profile of v2, /device:TPU:34, one launch (start us, length us, event | category | flops | bytes accessed | tf_op | source)
XLA Modules:
  0.0 311.2 jit_solution(3974747771876538418)
XLA Ops:
  0.0 7.4 %pack_rows.1 = bf16[512,8960]{1,0:T(8,128)(2,1)} custom-call(s32[8,64]{1,0:T(8,128)} %bitcast.20, bf16[64,7168]{1,0:T(8,128)(2,1)} %refs_1_), custom_call_target="tpu_custom_call" | custom-call | tf_op jit(solution)/shard_map/pack_rows/pallas_call | solution.py:63
  7.4 11.2 %all-to-all-start = ((bf16[64,8,8960]{2,1,0:T(8,128)(2,1)}), bf16[64,8,8960]{2,1,0:T(8,128)(2,1)}, u32[]{:S(2)}, u32[]{:S(2)}) async-start(bf16[64,8,8960]{2,1,0:T(8,128)(2,1)} %bitcast.12), calls=%async_computation | async-start | bytes 18350080 | tf_op jit(solution)/shard_map/all_to_all | solution.py:263
  18.6 0.1 collective-permute-start
  18.7 0.5 collective-permute-start.1
  19.2 0.1 collective-permute-start.2
  19.3 11.4 %collective-permute-done.g1 = bf16[3584,1024]{1,0:T(8,128)(2,1)} collective-permute-done((bf16[3584,1024]{1,0:T(8,128)(2,1)}, bf16[3584,1024]{1,0:T(8,128)(2,1)}, u32[]{:S(2)}, u32[]{:S(2)}) %collective-permute-start) | collective-permute-done | bytes 7340064 | tf_op jit(solution)/shard_map/ppermute | solution.py:275
  30.7 10.5 %collective-permute-done.1.u1 = bf16[3584,1024]{1,0:T(8,128)(2,1)} collective-permute-done((bf16[3584,1024]{1,0:T(8,128)(2,1)}, bf16[3584,1024]{1,0:T(8,128)(2,1)}, u32[]{:S(2)}, u32[]{:S(2)}) %collective-permute-start.1) | collective-permute-done | bytes 7340064 | tf_op jit(solution)/shard_map/ppermute | solution.py:275
  41.2 10.5 %collective-permute-done.2.d1 = bf16[1024,3584]{1,0:T(8,128)(2,1)} collective-permute-done((bf16[1024,3584]{1,0:T(8,128)(2,1)}, bf16[1024,3584]{1,0:T(8,128)(2,1)}, u32[]{:S(2)}, u32[]{:S(2)}) %collective-permute-start.2) | collective-permute-done | bytes 7340064 | tf_op jit(solution)/shard_map/ppermute | solution.py:275
  51.7 98.1 %all-to-all-done = bf16[64,8,8960]{2,1,0:T(8,128)(2,1)} async-done(((bf16[64,8,8960]{2,1,0:T(8,128)(2,1)}), bf16[64,8,8960]{2,1,0:T(8,128)(2,1)}, u32[]{:S(2)}, u32[]{:S(2)}) %all-to-all-start) | async-done | bytes 9175072 | tf_op jit(solution)/shard_map/all_to_all | solution.py:263
  149.9 44.7 %expert_ffn.1 = bf16[512,8960]{1,0:T(8,128)(2,1)} custom-call(s32[1]{0:T(128)} %bitcast.2.z_ref, bf16[512,8960]{1,0:T(8,128)(2,1)} %bitcast.4.x_ref.left_ref, bf16[512,8960]{1,0:T(8,128)(2,1)} %bitcast.4.x_ref.left_ref, bf16[3584,1024]{1,0:T(8,128)(2,1)} %bitcast.15, bf16[3584,1024]{1,0:T(8,128)(2,1)} %collective-permute-done.g1, ...), custom_call_target="tpu_custom_call" | custom-call | tf_op jit(solution)/shard_map/expert_ffn/pallas_call | solution.py:188
  194.6 109.3 %all_to_all.10 = bf16[64,8,8960]{2,1,0:T(8,128)(2,1)} all-to-all(bf16[64,8,8960]{2,1,0:T(8,128)(2,1)} %bitcast.13), channel_id=1, replica_groups=mesh['expert'=64,'zero'=2] {'expert'}, dimensions={0} | all-to-all | bytes 18350080 | tf_op jit(solution)/shard_map/all_to_all | solution.py:263
  303.9 7.4 %merge_rows.1 = bf16[64,7168]{1,0:T(8,128)(2,1)} custom-call(s32[8,64]{1,0:T(8,128)} %bitcast.21, f32[8,64]{1,0:T(8,128)} %bitcast.22, bf16[512,8960]{1,0:T(8,128)(2,1)} %bitcast.10, bf16[512,8960]{1,0:T(8,128)(2,1)} %bitcast.11), custom_call_target="tpu_custom_call" | custom-call | tf_op jit(solution)/shard_map/merge_rows/pallas_call | solution.py:245
Async XLA Ops:
  7.4 142.4 %all-to-all-start = ((bf16[64,8,8960]{2,1,0:T(8,128)(2,1)}), bf16[64,8,8960]{2,1,0:T(8,128)(2,1)}, u32[]{:S(2)}, u32[]{:S(2)}) async-start(bf16[64,8,8960]{2,1,0:T(8,128)(2,1)} %bitcast.12), calls=%async_computation | async-start | bytes 18350080 | tf_op jit(solution)/shard_map/all_to_all | solution.py:263
  18.6 12.1 %collective-permute-start = (bf16[3584,1024]{1,0:T(8,128)(2,1)}, bf16[3584,1024]{1,0:T(8,128)(2,1)}, u32[]{:S(2)}, u32[]{:S(2)}) collective-permute-start(bf16[3584,1024]{1,0:T(8,128)(2,1)} %bitcast.14), channel_id=1, source_target_pairs={{0,1},{1,0},{2,3},{3,2},{4,5},{5,4},{6,7},{7,6},{8,9},{9,8},{10,11... | collective-permute-start | bytes 22020104 | tf_op jit(solution)/shard_map/ppermute | solution.py:275
  18.7 22.5 %collective-permute-start.1 = (bf16[3584,1024]{1,0:T(8,128)(2,1)}, bf16[3584,1024]{1,0:T(8,128)(2,1)}, u32[]{:S(2)}, u32[]{:S(2)}) collective-permute-start(bf16[3584,1024]{1,0:T(8,128)(2,1)} %bitcast.16), channel_id=1, source_target_pairs={{0,1},{1,0},{2,3},{3,2},{4,5},{5,4},{6,7},{7,6},{8,9},{9,8},{10,11... | collective-permute-start | bytes 22020104 | tf_op jit(solution)/shard_map/ppermute | solution.py:275
  19.2 32.5 %collective-permute-start.2 = (bf16[1024,3584]{1,0:T(8,128)(2,1)}, bf16[1024,3584]{1,0:T(8,128)(2,1)}, u32[]{:S(2)}, u32[]{:S(2)}) collective-permute-start(bf16[1024,3584]{1,0:T(8,128)(2,1)} %bitcast.18), channel_id=1, source_target_pairs={{0,1},{1,0},{2,3},{3,2},{4,5},{5,4},{6,7},{7,6},{8,9},{9,8},{10,11... | collective-permute-start | bytes 22020104 | tf_op jit(solution)/shard_map/ppermute | solution.py:275
